TPU v7x, 32 devices: a whole 2x2x4 slice. The times are simulated.
32 devices in a mesh: chain: 2 (over y), cell: 4 (over z), col: 4 (over x, core).
Axes of the slice: x: 2, y: 2, z: 4, core: 2. Of those that a mesh axis runs over, the one named last changes fastest.
Arguments:
- grad: float32 [16384, 64], P(('chain', 'cell', 'col')), parts along dimension 0, may hold values from -6 to 6
- near_tiles: bfloat16 [4, 2, 2048, 2048], P('cell', None, 'col'), may hold values from -0.09375 to 0.09375
- tile_count: int32 [4], replicated, may hold values from 1 to 2
- near_offset: int32 [4], replicated, may hold values from -2 to 2, as said below
- far_src: int32 [4, 8], replicated, may hold values from 0 to 3
- far_count: int32 [4], replicated, may hold values from 1 to 8
- far_cores: float32 [4, 8, 64, 64], P('cell'), may hold values from -0.25 to 0.25
- basis_out: bfloat16 [8192, 64], P(('cell', 'col')), may hold values from -0.75 to 0.75
- basis_in: bfloat16 [8192, 64], P(('cell', 'col')), may hold values from -0.125 to 0.125
Outputs:
- step_block: float32 [16384, 64], P(('chain', 'cell', 'col')), parts along dimension 0
There are 2 independent parts, one for each index of `chain`. A program takes and returns all parts, laid end to end along the dimension named above; an argument that names none is the same for every part. Nothing has to cross between parts.
Inputs may be any that keep to these rules, and one draw needn't show every extreme that they name: c + near_offset[c] is a cluster of the chain, and near_offset[c] is never 0.
All inputs are finite; a program needn't handle non-finite values.
Results may differ from a plain program's by a relative error of at most 0.0035.
Values may be sent and summed in bfloat16 or wider, within the bound.
No kernel may reach another device: no remote copies, remote signals or barrier semaphores. Data moves between devices by JAX's collectives and lax.ppermute only.
A program may use at most 64 MiB of HBM per device.

v0:
```python
import jax
import jax.numpy as jnp
from jax import lax
from jax.sharding import PartitionSpec as P


def shifted(value, axis, by):
    devices = lax.axis_size(axis)
    pairs = [(i, i + by) for i in range(devices) if 0 <= i + by < devices]
    return lax.ppermute(value, axis, pairs)


def pick_offset(stacked, offset):
    position = offset + 2 - (offset > 0).astype(jnp.int32)
    return lax.dynamic_index_in_dim(stacked, position, 0, keepdims=False)


def coupling(table, sources, count, cores):
    picked = jnp.take(table, sources, axis=0)
    slots = jnp.arange(cores.shape[0], dtype=jnp.int32)
    masked = jnp.where((slots < count)[:, None, None], cores, jnp.zeros_like(cores))
    return jnp.einsum("kab,kbw->aw", masked, picked, precision=lax.Precision.HIGHEST)


def body(
    grad, near_tiles, tile_count, near_offset, far_src, far_count, far_cores, basis_out, basis_in
):
    owner = lax.axis_index("cell")
    rounded = grad.astype(jnp.bfloat16)
    offset = near_offset[owner]
    steps_list = (-2, -1, 1, 2)
    whole = lax.all_gather(rounded, "col", axis=0, tiled=True)
    moved = [shifted(whole, "cell", -step) for step in steps_list]
    beside = pick_offset(jnp.stack(moved), offset)
    tiles = near_tiles[0]
    own_term = jnp.dot(tiles[0], whole, preferred_element_type=jnp.float32)
    other_term = jnp.dot(tiles[1], beside, preferred_element_type=jnp.float32)
    near = own_term + jnp.where(tile_count[owner] == 2, other_term, jnp.zeros_like(other_term))
    partial_proj = lax.dot_general(
        basis_in, rounded, (((0,), (0,)), ((), ())), preferred_element_type=jnp.float32
    )
    sources = far_src[owner]
    count = far_count[owner]
    cores = far_cores[0]
    proj = lax.psum(partial_proj, "col")
    table = lax.all_gather(proj[None], "cell", axis=0, tiled=True)
    core_block = coupling(table, sources, count, cores).astype(jnp.bfloat16)
    far = jnp.dot(basis_out, core_block, preferred_element_type=jnp.float32)
    return near + far


def solution(mesh):
    placed = (
        P(("chain", "cell", "col"), None),
        P("cell", None, "col", None),
        P(),
        P(),
        P(),
        P(),
        P("cell", None, None, None),
        P(("cell", "col"), None),
        P(("cell", "col"), None),
    )
    return jax.shard_map(
        body,
        mesh=mesh,
        in_specs=placed,
        out_specs=P(("chain", "cell", "col"), None),
        check_vma=False,
    )
```

profile of v0, /device:TPU:0, one launch (start us, length us, event | category | flops | bytes accessed | tf_op | source)
XLA Modules:
  0.0 60.8 jit_solution(2780922674257491303)
XLA Ops:
  0.0 0.0 copy-start
  0.0 0.9 %convert_element_type.10 = bf16[512,64]{0,1:T(8,128)(2,1)S(1)} convert(f32[512,64]{0,1:T(8,128)} %param.9) | non-fusion elementwise | flops 32768 | bytes 196608 | tf_op jit(solution)/shard_map/convert_element_type | solution.py:29
  1.0 7.2 %all_gather.6 = bf16[2048,64]{0,1:T(8,128)(2,1)S(1)} all-gather(bf16[512,64]{0,1:T(8,128)(2,1)S(1)} %convert_element_type.10), channel_id=1, replica_groups=mesh['chain'=2,'cell'=4,'col'=4] {'col'}, dimensions={0}, use_global_device_ids=true | all-gather | bytes 327680 | tf_op jit(solution)/shard_map/all_gather | solution.py:32
  8.2 4.5 %collective-permute-start = (bf16[2048,64]{0,1:T(8,128)(2,1)S(1)}, bf16[2048,64]{0,1:T(8,128)(2,1)S(1)}, u32[]{:S(2)}, u32[]{:S(2)}) collective-permute-start(bf16[2048,64]{0,1:T(8,128)(2,1)S(1)} %all_gather.6), channel_id=1, source_target_pairs={{0,8},{4,12},{1,9},{5,13},{2,10},{6,14},{3,11},{7,15},{16,24},{20,... | collective-permute-start | bytes 786440 | tf_op jit(solution)/shard_map/ppermute | solution.py:10
  12.7 3.5 %collective-permute-start.1 = (bf16[2048,64]{0,1:T(8,128)(2,1)S(1)}, bf16[2048,64]{0,1:T(8,128)(2,1)S(1)}, u32[]{:S(2)}, u32[]{:S(2)}) collective-permute-start(bf16[2048,64]{0,1:T(8,128)(2,1)S(1)} %all_gather.6), channel_id=1, source_target_pairs={{0,4},{4,8},{8,12},{1,5},{5,9},{9,13},{2,6},{6,10},{10,14},{3,7},{... | collective-permute-start | bytes 786440 | tf_op jit(solution)/shard_map/ppermute | solution.py:10
  16.2 1.3 %collective-permute-start.2 = (bf16[2048,64]{0,1:T(8,128)(2,1)S(1)}, bf16[2048,64]{0,1:T(8,128)(2,1)S(1)}, u32[]{:S(2)}, u32[]{:S(2)}) collective-permute-start(bf16[2048,64]{0,1:T(8,128)(2,1)S(1)} %all_gather.6), channel_id=1, source_target_pairs={{4,0},{8,4},{12,8},{5,1},{9,5},{13,9},{6,2},{10,6},{14,10},{7,3},{... | collective-permute-start | bytes 786440 | tf_op jit(solution)/shard_map/ppermute | solution.py:10
  17.5 1.3 %collective-permute-start.3 = (bf16[2048,64]{0,1:T(8,128)(2,1)S(1)}, bf16[2048,64]{0,1:T(8,128)(2,1)S(1)}, u32[]{:S(2)}, u32[]{:S(2)}) collective-permute-start(bf16[2048,64]{0,1:T(8,128)(2,1)S(1)} %all_gather.6), channel_id=1, source_target_pairs={{8,0},{12,4},{9,1},{13,5},{10,2},{14,6},{11,3},{15,7},{24,16},{28,... | collective-permute-start | bytes 786440 | tf_op jit(solution)/shard_map/ppermute | solution.py:10
  18.8 1.2 %dynamic_slice.19 = s32[1]{0:T(128)} dynamic-slice(s32[4]{0:T(128)} %param.14, s32[]{:T(128)S(6)} %select_n.45), dynamic_slice_sizes={1} | dynamic-slice | bytes 12 | tf_op jit(solution)/shard_map/dynamic_slice | solution.py:43
  20.1 0.7 %fusion.30 = s32[8]{0:T(128)S(1)} fusion(s32[4,8]{1,0:T(4,128)} %param.13, s32[]{:T(128)S(6)} %select_n.45), kind=kLoop, calls=%fused_computation.35 | loop fusion | flops 24 | bytes 68 | tf_op jit(solution)/shard_map/jit(_take)/jit(_where)/select_n | solution.py:19
  20.8 1.3 %compare_and_fusion = (pred[8]{0:T(512)(128)(4,1)S(1)}, pred[8]{0:T(512)(128)(4,1)S(1)}) fusion(s32[4,8]{1,0:T(4,128)} %param.13, s32[]{:T(128)S(6)} %select_n.45, s32[]{:T(128)} %bitcast.10), kind=kLoop, calls=%fused_computation.32 | loop fusion | flops 56 | bytes 56 | tf_op jit(solution)/shard_map/jit(_take)/and | solution.py:19
  22.1 1.0 %convolution_bitcast_fusion.1 = f32[1,64,64]{2,1,0:T(8,128)S(1)} fusion(bf16[512,64]{0,1:T(8,128)(2,1)} %param.17, bf16[512,64]{0,1:T(8,128)(2,1)S(1)} %convert_element_type.10), kind=kOutput, calls=%fused_computation.12 | convolution fusion | flops 4194304 | bytes 147456 | tf_op jit(solution)/shard_map/dot_general | solution.py:39
  23.1 11.4 %psum.7 = f32[1,64,64]{2,1,0:T(8,128)S(1)} all-reduce(f32[1,64,64]{2,1,0:T(8,128)S(1)} %convolution_bitcast_fusion.1), channel_id=1, replica_groups=mesh['chain'=2,'cell'=4,'col'=4] {'col'}, use_global_device_ids=true, to_apply=%region_0.1 | all-reduce | flops 4096 | bytes 32768 | tf_op jit(solution)/shard_map/psum | solution.py:45
  34.5 14.3 %all_gather.7 = f32[4,64,64]{2,1,0:T(8,128)S(1)} all-gather(f32[1,64,64]{2,1,0:T(8,128)S(1)} %psum.7), channel_id=1, replica_groups=mesh['chain'=2,'cell'=4,'col'=4] {'cell'}, dimensions={0}, use_global_device_ids=true | all-gather | bytes 81920 | tf_op jit(solution)/shard_map/all_gather | solution.py:46
  48.8 0.6 gather_fusion
  49.3 1.4 %fusion.18 = bf16[64,64]{1,0:T(8,128)(2,1)S(1)} fusion(f32[1,8,64,64]{3,2,1,0:T(8,128)} %param.15, f32[8,64,64]{2,1,0:T(8,128)S(1)} %gather_fusion, pred[8]{0:T(512)(128)(4,1)S(1)} %get-tuple-element.5, pred[8]{0:T(512)(128)(4,1)S(1)} %get-tuple-element.6), kind=kOutput, calls=%fused_computation.14 | convolution fusion | flops 25235456 | bytes 270352 | tf_op jit(solution)/shard_map/kab,kbw->aw/dot_general | solution.py:22
  50.8 1.2 %dynamic_slice.17 = s32[1]{0:T(128)} dynamic-slice(s32[4]{0:T(128)} %param.12, s32[]{:T(128)S(6)} %select_n.45), dynamic_slice_sizes={1} | dynamic-slice | bytes 12 | tf_op jit(solution)/shard_map/dynamic_slice | solution.py:30
  53.3 1.3 %dynamic_slice.16 = s32[1]{0:T(128)} dynamic-slice(s32[4]{0:T(128)} %param.11, s32[]{:T(128)S(6)} %select_n.45), dynamic_slice_sizes={1} | dynamic-slice | bytes 12 | tf_op jit(solution)/shard_map/dynamic_slice | solution.py:38
  55.2 0.0 copy-done
  55.2 0.2 convolution_bitcast_fusion
  55.4 0.0 collective-permute-done
  55.4 0.0 collective-permute-done.1
  55.4 0.0 collective-permute-done.2
  55.4 0.0 collective-permute-done.3
  55.4 2.4 %fusion.15 = f32[512,64]{0,1:T(8,128)S(1)} fusion(bf16[1,2,512,2048]{3,2,1,0:T(8,128)(2,1)} %param.10, s32[]{:T(128)S(6)} %select_n.47, bf16[1,2048,64]{1,2,0:T(8,128)(2,1)S(1)} %bitcast.48, bf16[1,2048,64]{1,2,0:T(8,128)(2,1)S(1)} %bitcast.49, bf16[1,2048,64]{1,2,0:T(8,128)(2,1)S(1)} %bitcast.50, bf16[1,2048,64]{1,2,0:T(8,128)(2,1)S(1)} %bitcast.51, ...), kind=kOutput, calls=%fused_computation.10 | convolution fusion | flops 134643712 | bytes 3277316 | tf_op jit(solution)/shard_map/dot_general | solution.py:37
  57.8 3.0 %fusion.9 = f32[512,64]{0,1:T(8,128)} fusion(f32[512,64]{0,1:T(8,128)S(1)} %convolution_bitcast_fusion, f32[512,64]{0,1:T(8,128)S(1)} %fusion.15, bf16[2048,64]{0,1:T(8,128)(2,1)S(1)} %all_gather.6, bf16[1,2,512,2048]{3,2,1,0:T(8,128)(2,1)} %param.10), kind=kOutput, calls=%fused_computation.8 | convolution fusion | flops 134283264 | bytes 2752512 | tf_op jit(solution)/shard_map/dot_general | solution.py:36
  (1 shorter events, 0.0 us)
Async XLA Ops:
  0.0 55.2 %copy-start = (bf16[512,64]{0,1:T(8,128)(2,1)S(1)}, bf16[512,64]{0,1:T(8,128)(2,1)}, u32[]{:S(2)}) copy-start(bf16[512,64]{0,1:T(8,128)(2,1)} %param.16) | copy-start | bytes 196612
  8.2 47.2 %collective-permute-start = (bf16[2048,64]{0,1:T(8,128)(2,1)S(1)}, bf16[2048,64]{0,1:T(8,128)(2,1)S(1)}, u32[]{:S(2)}, u32[]{:S(2)}) collective-permute-start(bf16[2048,64]{0,1:T(8,128)(2,1)S(1)} %all_gather.6), channel_id=1, source_target_pairs={{0,8},{4,12},{1,9},{5,13},{2,10},{6,14},{3,11},{7,15},{16,24},{20,... | collective-permute-start | bytes 786440 | tf_op jit(solution)/shard_map/ppermute | solution.py:10
  12.7 42.7 %collective-permute-start.1 = (bf16[2048,64]{0,1:T(8,128)(2,1)S(1)}, bf16[2048,64]{0,1:T(8,128)(2,1)S(1)}, u32[]{:S(2)}, u32[]{:S(2)}) collective-permute-start(bf16[2048,64]{0,1:T(8,128)(2,1)S(1)} %all_gather.6), channel_id=1, source_target_pairs={{0,4},{4,8},{8,12},{1,5},{5,9},{9,13},{2,6},{6,10},{10,14},{3,7},{... | collective-permute-start | bytes 786440 | tf_op jit(solution)/shard_map/ppermute | solution.py:10
  16.2 39.2 %collective-permute-start.2 = (bf16[2048,64]{0,1:T(8,128)(2,1)S(1)}, bf16[2048,64]{0,1:T(8,128)(2,1)S(1)}, u32[]{:S(2)}, u32[]{:S(2)}) collective-permute-start(bf16[2048,64]{0,1:T(8,128)(2,1)S(1)} %all_gather.6), channel_id=1, source_target_pairs={{4,0},{8,4},{12,8},{5,1},{9,5},{13,9},{6,2},{10,6},{14,10},{7,3},{... | collective-permute-start | bytes 786440 | tf_op jit(solution)/shard_map/ppermute | solution.py:10
  17.5 37.9 %collective-permute-start.3 = (bf16[2048,64]{0,1:T(8,128)(2,1)S(1)}, bf16[2048,64]{0,1:T(8,128)(2,1)S(1)}, u32[]{:S(2)}, u32[]{:S(2)}) collective-permute-start(bf16[2048,64]{0,1:T(8,128)(2,1)S(1)} %all_gather.6), channel_id=1, source_target_pairs={{8,0},{12,4},{9,1},{13,5},{10,2},{14,6},{11,3},{15,7},{24,16},{28,... | collective-permute-start | bytes 786440 | tf_op jit(solution)/shard_map/ppermute | solution.py:10
where the time goes:
time: 61.3 us; the launch traced here: 60.8 us
  blocking collectives  32.9 us (54%)
  starting transfers between devices  10.6 us (17%)
  matrix products  7.95 us (13%)
  local copies, waits for them, and re-layouts  4.33 us (7%)
  other arithmetic  2.98 us (5%)
  between operations  2.04 us (3%)
    all_gather x1, blocking collectives, body(): table = lax.all_gather(proj[None], 'cell', axis=0, tiled=True)  14.3 us
    psum x1, blocking collectives, body(): proj = lax.psum(partial_proj, 'col')  11.4 us
    ppermute x4, starting transfers between devices, shifted(): return lax.ppermute(value, axis, pairs)  10.6 us
    all_gather x1, blocking collectives, body(): whole = lax.all_gather(rounded, 'col', axis=0, tiled=True)  7.22 us
    dot_general x1, matrix products, body(): own_term = jnp.dot(tiles[0], whole, preferred_element_type=jnp.float32)  3.01 us
    dot_general x1, matrix products, body(): other_term = jnp.dot(tiles[1], beside, preferred_element_type=jnp.float32)  2.36 us
    dot_general x1, matrix products, coupling(): jnp.einsum('kab,kbw->aw', masked, picked, precision=lax.Precision.HIGHEST)  1.42 us
    and x1, other arithmetic, coupling(): picked = jnp.take(table, sources, axis=0)  1.34 us
  transfers between devices with their start and end apart: 4, of which 0 were waited for; matrix products, arithmetic and copies ran while one was open for 15% of the time, Pallas kernels for 0%

commit v1 on v0

--- a/solution.py
+++ b/solution.py
@@ -2,6 +2,12 @@
 import jax.numpy as jnp
 from jax import lax
 from jax.sharding import PartitionSpec as P
+
+
+def in_order(parts, dim):
+    lengths = list(parts.shape[1:])
+    lengths[dim] *= parts.shape[0]
+    return jnp.moveaxis(parts, 0, dim).reshape(lengths)
 
 
 def shifted(value, axis, by):
@@ -29,7 +35,19 @@
     rounded = grad.astype(jnp.bfloat16)
     offset = near_offset[owner]
     steps_list = (-2, -1, 1, 2)
-    whole = lax.all_gather(rounded, "col", axis=0, tiled=True)
+    count_2 = lax.axis_size("col")
+    pairs_2 = [(i_2, (i_2 + 1) % count_2) for i_2 in range(count_2)]
+    back = [(b, a) for a, b in pairs_2]
+    lower, upper = ([], [])
+    for step_2 in range(count_2 - 1):
+        if step_2 % 2 == 0:
+            lower.append(lax.ppermute(lower[-1] if lower else rounded, "col", pairs_2))
+        else:
+            upper.append(lax.ppermute(upper[-1] if upper else rounded, "col", back))
+    blocks = jnp.stack([*lower[::-1], rounded, *upper])
+    shift = lax.axis_index("col") - len(lower)
+    blocks = blocks[(jnp.arange(count_2) - shift) % count_2]
+    whole = in_order(blocks, 0)
     moved = [shifted(whole, "cell", -step) for step in steps_list]
     beside = pick_offset(jnp.stack(moved), offset)
     tiles = near_tiles[0]

time: 61.3 us -> 65.2 us (1.064); the launches traced: 60.8 us -> 64 us
  blocking collectives: 32.9 us -> 24.6 us
  waiting for transfers between devices: 0.01 us -> 6.15 us
  starting transfers between devices: 10.6 us -> 14.2 us
  other arithmetic: 2.98 us -> 3.95 us
    all_gather x1 -> x0, blocking collectives: 7.22 us -> none  [body(): whole = lax.all_gather(rounded, 'col', axis=0, tiled=True)]
    ppermute x4, waiting for transfers between devices: 0.01 us -> 3.81 us  [shifted(): return lax.ppermute(value, axis, pairs)]
    ppermute x0 -> x3, starting transfers between devices: none -> 2.58 us  [the longest x1 1.98 us: body(): upper.append(lax.ppermute(upper[-1] if upper else rounded, 'col', back))]
    ppermute x0 -> x3, waiting for transfers between devices: none -> 2.34 us  [the longest x2 2.33 us: body(): lower.append(lax.ppermute(lower[-1] if lower else rounded, 'col', pairs_2))]
    ppermute x4, starting transfers between devices: 10.6 us -> 11.6 us  [shifted(): return lax.ppermute(value, axis, pairs)]
    another operation x0 -> x2, other arithmetic: none -> 0.95 us  [body(): blocks = jnp.stack([*lower[::-1], rounded, *upper])]
  transfers between devices with their start and end apart: 4 -> 7, of which waited for: 0 -> 2; matrix products, arithmetic and copies ran while one was open for 15% -> 15% of each run, Pallas kernels for 0% -> 0%
where the time goes in v1:
time: 65.2 us; the launch traced here: 64 us
  blocking collectives  24.6 us (38%)
  starting transfers between devices  14.2 us (22%)
  matrix products  7.94 us (12%)
  waiting for transfers between devices  6.15 us (9%)
  local copies, waits for them, and re-layouts  4.96 us (8%)
  other arithmetic  3.95 us (6%)
  between operations  2.17 us (3%)
    all_gather x1, blocking collectives, body(): table = lax.all_gather(proj[None], 'cell', axis=0, tiled=True)  13.8 us
    ppermute x4, starting transfers between devices, shifted(): return lax.ppermute(value, axis, pairs)  11.6 us
    psum x1, blocking collectives, body(): proj = lax.psum(partial_proj, 'col')  10.8 us
    ppermute x4, waiting for transfers between devices, shifted(): return lax.ppermute(value, axis, pairs)  3.81 us
    dot_general x1, matrix products, body(): own_term = jnp.dot(tiles[0], whole, preferred_element_type=jnp.float32)  3.02 us
    dot_general x1, matrix products, body(): other_term = jnp.dot(tiles[1], beside, preferred_element_type=jnp.float32)  2.35 us
    ppermute x2, waiting for transfers between devices, body(): lower.append(lax.ppermute(lower[-1] if lower else rounded, 'col', pairs_2))  2.33 us
    ppermute x1, starting transfers between devices, body(): upper.append(lax.ppermute(upper[-1] if upper else rounded, 'col', back))  1.98 us
  transfers between devices with their start and end apart: 7, of which 2 were waited for; matrix products, arithmetic and copies ran while one was open for 15% of the time, Pallas kernels for 0%

profile of v1, /device:TPU:0, one launch (start us, length us, event | category | flops | bytes accessed | tf_op | source)
XLA Modules:
  0.0 64.0 jit_solution(10837949486279774720)
XLA Ops:
  0.0 0.0 copy-start
  0.0 0.9 %convert_element_type.10 = bf16[512,64]{0,1:T(8,128)(2,1)S(1)} convert(f32[512,64]{0,1:T(8,128)} %param.9) | non-fusion elementwise | flops 32768 | bytes 196608 | tf_op jit(solution)/shard_map/convert_element_type | solution.py:35
  1.0 0.5 collective-permute-start
  1.5 2.0 %collective-permute-start.2 = (bf16[512,64]{0,1:T(8,128)(2,1)S(1)}, bf16[512,64]{0,1:T(8,128)(2,1)S(1)}, u32[]{:S(2)}, u32[]{:S(2)}) collective-permute-start(bf16[512,64]{0,1:T(8,128)(2,1)S(1)} %convert_element_type.10), channel_id=1, source_target_pairs={{1,0},{2,1},{3,2},{0,3},{5,4},{6,5},{7,6},{4,7},{9,8},{10,9},{11,1... | collective-permute-start | bytes 196616 | tf_op jit(solution)/shard_map/ppermute | solution.py:46
  3.5 0.9 %convert_bitcast_fusion = bf16[1,512,64]{1,2,0:T(8,128)(2,1)S(1)} fusion(f32[512,64]{0,1:T(8,128)} %param.9), kind=kLoop, calls=%fused_computation.49 | loop fusion | flops 32768 | bytes 196608 | tf_op jit(solution)/shard_map/stack | solution.py:47
  4.4 1.2 %dynamic_slice.19 = s32[1]{0:T(128)} dynamic-slice(s32[4]{0:T(128)} %param.14, s32[]{:T(128)S(6)} %select_n.69), dynamic_slice_sizes={1} | dynamic-slice | bytes 12 | tf_op jit(solution)/shard_map/dynamic_slice | solution.py:61
  5.7 0.7 %fusion.32 = s32[8]{0:T(128)S(1)} fusion(s32[4,8]{1,0:T(4,128)} %param.13, s32[]{:T(128)S(6)} %select_n.69), kind=kLoop, calls=%fused_computation.43 | loop fusion | flops 24 | bytes 68 | tf_op jit(solution)/shard_map/jit(_take)/jit(_where)/select_n | solution.py:25
  6.4 1.0 %convolution_bitcast_fusion = f32[1,64,64]{2,1,0:T(8,128)S(1)} fusion(bf16[512,64]{0,1:T(8,128)(2,1)} %param.17, bf16[512,64]{0,1:T(8,128)(2,1)S(1)} %convert_element_type.10), kind=kOutput, calls=%fused_computation.12 | convolution fusion | flops 4194304 | bytes 147456 | tf_op jit(solution)/shard_map/dot_general | solution.py:57
  7.3 10.8 %psum.7 = f32[1,64,64]{2,1,0:T(8,128)S(1)} all-reduce(f32[1,64,64]{2,1,0:T(8,128)S(1)} %convolution_bitcast_fusion), channel_id=1, replica_groups=mesh['chain'=2,'cell'=4,'col'=4] {'col'}, use_global_device_ids=true, to_apply=%region_0.1 | all-reduce | flops 4096 | bytes 32768 | tf_op jit(solution)/shard_map/psum | solution.py:63
  18.2 13.8 %all_gather.3 = f32[4,64,64]{2,1,0:T(8,128)S(1)} all-gather(f32[1,64,64]{2,1,0:T(8,128)S(1)} %psum.7), channel_id=1, replica_groups=mesh['chain'=2,'cell'=4,'col'=4] {'cell'}, dimensions={0}, use_global_device_ids=true | all-gather | bytes 81920 | tf_op jit(solution)/shard_map/all_gather | solution.py:64
  32.0 0.6 gather_fusion.1
  32.6 0.0 collective-permute-done
  32.6 0.1 collective-permute-start.1
  32.6 1.3 %compare_and_fusion = (pred[8]{0:T(512)(128)(4,1)S(1)}, pred[8]{0:T(512)(128)(4,1)S(1)}) fusion(s32[4,8]{1,0:T(4,128)} %param.13, s32[]{:T(128)S(6)} %select_n.69, s32[]{:T(128)} %bitcast.14), kind=kLoop, calls=%fused_computation.37 | loop fusion | flops 56 | bytes 56 | tf_op jit(solution)/shard_map/jit(_take)/and | solution.py:25
  34.0 0.0 collective-permute-done.2
  34.0 2.3 %collective-permute-done.1 = bf16[512,64]{0,1:T(8,128)(2,1)S(1)} collective-permute-done((bf16[512,64]{0,1:T(8,128)(2,1)S(1)}, bf16[512,64]{0,1:T(8,128)(2,1)S(1)}, u32[]{:S(2)}, u32[]{:S(2)}) %collective-permute-start.1) | collective-permute-done | bytes 65568 | tf_op jit(solution)/shard_map/ppermute | solution.py:44
  36.3 0.6 gather_fusion
  36.9 1.3 %collective-permute-start.6 = (bf16[2048,64]{0,1:T(8,128)(2,1)S(1)}, bf16[2048,64]{0,1:T(8,128)(2,1)S(1)}, u32[]{:S(2)}, u32[]{:S(2)}) collective-permute-start(bf16[2048,64]{0,1:T(8,128)(2,1)S(1)} %bitcast.56), channel_id=1, source_target_pairs={{8,0},{12,4},{9,1},{13,5},{10,2},{14,6},{11,3},{15,7},{24,16},{28,... | collective-permute-start | bytes 786440 | tf_op jit(solution)/shard_map/ppermute | solution.py:16
  38.2 5.5 %collective-permute-start.3 = (bf16[2048,64]{0,1:T(8,128)(2,1)S(1)}, bf16[2048,64]{0,1:T(8,128)(2,1)S(1)}, u32[]{:S(2)}, u32[]{:S(2)}) collective-permute-start(bf16[2048,64]{0,1:T(8,128)(2,1)S(1)} %bitcast.57), channel_id=1, source_target_pairs={{0,8},{4,12},{1,9},{5,13},{2,10},{6,14},{3,11},{7,15},{16,24},{20,... | collective-permute-start | bytes 786440 | tf_op jit(solution)/shard_map/ppermute | solution.py:16
  43.7 3.5 %collective-permute-start.4 = (bf16[2048,64]{0,1:T(8,128)(2,1)S(1)}, bf16[2048,64]{0,1:T(8,128)(2,1)S(1)}, u32[]{:S(2)}, u32[]{:S(2)}) collective-permute-start(bf16[2048,64]{0,1:T(8,128)(2,1)S(1)} %bitcast.58), channel_id=1, source_target_pairs={{0,4},{4,8},{8,12},{1,5},{5,9},{9,13},{2,6},{6,10},{10,14},{3,7},{... | collective-permute-start | bytes 786440 | tf_op jit(solution)/shard_map/ppermute | solution.py:16
  47.3 1.3 %collective-permute-start.5 = (bf16[2048,64]{0,1:T(8,128)(2,1)S(1)}, bf16[2048,64]{0,1:T(8,128)(2,1)S(1)}, u32[]{:S(2)}, u32[]{:S(2)}) collective-permute-start(bf16[2048,64]{0,1:T(8,128)(2,1)S(1)} %bitcast.59), channel_id=1, source_target_pairs={{4,0},{8,4},{12,8},{5,1},{9,5},{13,9},{6,2},{10,6},{14,10},{7,3},{... | collective-permute-start | bytes 786440 | tf_op jit(solution)/shard_map/ppermute | solution.py:16
  48.6 1.4 %fusion.18 = bf16[64,64]{1,0:T(8,128)(2,1)S(1)} fusion(f32[1,8,64,64]{3,2,1,0:T(8,128)} %param.15, f32[8,64,64]{2,1,0:T(8,128)S(1)} %gather_fusion.1, pred[8]{0:T(512)(128)(4,1)S(1)} %get-tuple-element.5, pred[8]{0:T(512)(128)(4,1)S(1)} %get-tuple-element.6), kind=kOutput, calls=%fused_computation.14 | convolution fusion | flops 25235456 | bytes 270352 | tf_op jit(solution)/shard_map/kab,kbw->aw/dot_general | solution.py:28
  50.0 1.2 %dynamic_slice.17 = s32[1]{0:T(128)} dynamic-slice(s32[4]{0:T(128)} %param.12, s32[]{:T(128)S(6)} %select_n.69), dynamic_slice_sizes={1} | dynamic-slice | bytes 12 | tf_op jit(solution)/shard_map/dynamic_slice | solution.py:36
  52.5 1.3 %dynamic_slice.16 = s32[1]{0:T(128)} dynamic-slice(s32[4]{0:T(128)} %param.11, s32[]{:T(128)S(6)} %select_n.69), dynamic_slice_sizes={1} | dynamic-slice | bytes 12 | tf_op jit(solution)/shard_map/dynamic_slice | solution.py:56
  54.6 0.0 copy-done
  54.6 0.2 fusion.36
  54.7 0.0 collective-permute-done.6
  54.8 0.0 collective-permute-done.3
  54.8 0.0 collective-permute-done.4
  54.8 3.8 %collective-permute-done.5 = bf16[2048,64]{0,1:T(8,128)(2,1)S(1)} collective-permute-done((bf16[2048,64]{0,1:T(8,128)(2,1)S(1)}, bf16[2048,64]{0,1:T(8,128)(2,1)S(1)}, u32[]{:S(2)}, u32[]{:S(2)}) %collective-permute-start.5) | collective-permute-done | bytes 262176 | tf_op jit(solution)/shard_map/ppermute | solution.py:16
  58.6 2.4 %fusion.15 = f32[64,512]{1,0:T(8,128)S(1)} fusion(bf16[1,2,512,2048]{3,2,1,0:T(8,128)(2,1)} %param.10, s32[]{:T(128)S(6)} %select_n.71, bf16[1,2048,64]{1,2,0:T(8,128)(2,1)S(1)} %bitcast.65, bf16[1,2048,64]{1,2,0:T(8,128)(2,1)S(1)} %bitcast.66, bf16[1,2048,64]{1,2,0:T(8,128)(2,1)S(1)} %bitcast.67, bf16[1,2048,64]{1,2,0:T(8,128)(2,1)S(1)} %bitcast.64, ...), kind=kOutput, calls=%fused_computation.11 | convolution fusion | flops 134643712 | bytes 3277316 | tf_op jit(solution)/shard_map/dot_general | solution.py:55
  60.9 3.0 %fusion.12 = f32[512,64]{0,1:T(8,128)} fusion(f32[64,512]{1,0:T(8,128)S(1)} %fusion.36, f32[64,512]{1,0:T(8,128)S(1)} %fusion.15, bf16[2048,64]{0,1:T(8,128)(2,1)S(1)} %bitcast.60, bf16[1,2,512,2048]{3,2,1,0:T(8,128)(2,1)} %param.10), kind=kOutput, calls=%fused_computation.10 | convolution fusion | flops 134283264 | bytes 2752512 | tf_op jit(solution)/shard_map/dot_general | solution.py:54
  (5 shorter events, 0.1 us)
Async XLA Ops:
  0.0 54.6 %copy-start = (bf16[512,64]{0,1:T(8,128)(2,1)S(1)}, bf16[512,64]{0,1:T(8,128)(2,1)}, u32[]{:S(2)}) copy-start(bf16[512,64]{0,1:T(8,128)(2,1)} %param.16) | copy-start | bytes 196612
  1.0 31.6 %collective-permute-start = (bf16[512,64]{0,1:T(8,128)(2,1)S(1)}, bf16[512,64]{0,1:T(8,128)(2,1)S(1)}, u32[]{:S(2)}, u32[]{:S(2)}) collective-permute-start(bf16[512,64]{0,1:T(8,128)(2,1)S(1)} %convert_element_type.10), channel_id=1, source_target_pairs={{0,1},{1,2},{2,3},{3,0},{4,5},{5,6},{6,7},{7,4},{8,9},{9,10},{10,1... | collective-permute-start | bytes 196616 | tf_op jit(solution)/shard_map/ppermute | solution.py:44
  1.5 32.5 %collective-permute-start.2 = (bf16[512,64]{0,1:T(8,128)(2,1)S(1)}, bf16[512,64]{0,1:T(8,128)(2,1)S(1)}, u32[]{:S(2)}, u32[]{:S(2)}) collective-permute-start(bf16[512,64]{0,1:T(8,128)(2,1)S(1)} %convert_element_type.10), channel_id=1, source_target_pairs={{1,0},{2,1},{3,2},{0,3},{5,4},{6,5},{7,6},{4,7},{9,8},{10,9},{11,1... | collective-permute-start | bytes 196616 | tf_op jit(solution)/shard_map/ppermute | solution.py:46
  32.6 3.7 %collective-permute-start.1 = (bf16[512,64]{0,1:T(8,128)(2,1)S(1)}, bf16[512,64]{0,1:T(8,128)(2,1)S(1)}, u32[]{:S(2)}, u32[]{:S(2)}) collective-permute-start(bf16[512,64]{0,1:T(8,128)(2,1)S(1)} %collective-permute-done), channel_id=1, source_target_pairs={{0,1},{1,2},{2,3},{3,0},{4,5},{5,6},{6,7},{7,4},{8,9},{9,10},{10,1... | collective-permute-start | bytes 196616 | tf_op jit(solution)/shard_map/ppermute | solution.py:44
  36.9 17.8 %collective-permute-start.6 = (bf16[2048,64]{0,1:T(8,128)(2,1)S(1)}, bf16[2048,64]{0,1:T(8,128)(2,1)S(1)}, u32[]{:S(2)}, u32[]{:S(2)}) collective-permute-start(bf16[2048,64]{0,1:T(8,128)(2,1)S(1)} %bitcast.56), channel_id=1, source_target_pairs={{8,0},{12,4},{9,1},{13,5},{10,2},{14,6},{11,3},{15,7},{24,16},{28,... | collective-permute-start | bytes 786440 | tf_op jit(solution)/shard_map/ppermute | solution.py:16
  38.2 16.5 %collective-permute-start.3 = (bf16[2048,64]{0,1:T(8,128)(2,1)S(1)}, bf16[2048,64]{0,1:T(8,128)(2,1)S(1)}, u32[]{:S(2)}, u32[]{:S(2)}) collective-permute-start(bf16[2048,64]{0,1:T(8,128)(2,1)S(1)} %bitcast.57), channel_id=1, source_target_pairs={{0,8},{4,12},{1,9},{5,13},{2,10},{6,14},{3,11},{7,15},{16,24},{20,... | collective-permute-start | bytes 786440 | tf_op jit(solution)/shard_map/ppermute | solution.py:16
  43.7 11.0 %collective-permute-start.4 = (bf16[2048,64]{0,1:T(8,128)(2,1)S(1)}, bf16[2048,64]{0,1:T(8,128)(2,1)S(1)}, u32[]{:S(2)}, u32[]{:S(2)}) collective-permute-start(bf16[2048,64]{0,1:T(8,128)(2,1)S(1)} %bitcast.58), channel_id=1, source_target_pairs={{0,4},{4,8},{8,12},{1,5},{5,9},{9,13},{2,6},{6,10},{10,14},{3,7},{... | collective-permute-start | bytes 786440 | tf_op jit(solution)/shard_map/ppermute | solution.py:16
  47.3 11.3 %collective-permute-start.5 = (bf16[2048,64]{0,1:T(8,128)(2,1)S(1)}, bf16[2048,64]{0,1:T(8,128)(2,1)S(1)}, u32[]{:S(2)}, u32[]{:S(2)}) collective-permute-start(bf16[2048,64]{0,1:T(8,128)(2,1)S(1)} %bitcast.59), channel_id=1, source_target_pairs={{4,0},{8,4},{12,8},{5,1},{9,5},{13,9},{6,2},{10,6},{14,10},{7,3},{... | collective-permute-start | bytes 786440 | tf_op jit(solution)/shard_map/ppermute | solution.py:16
